TPU v7x, 128 devices: a whole 4x4x4 slice. The times are simulated.
128 devices in a mesh: grp: 8 (over x, core), dev: 16 (over z, y).
Axes of the slice: x: 4, y: 4, z: 4, core: 2. Of those that a mesh axis runs over, the one named last changes fastest.
Arguments:
- residual: bfloat16 [16384, 2048], P(('grp', 'dev')), may hold values from -3 to 3
- queries: bfloat16 [16384, 1024], P(('grp', 'dev')), may hold values from -9 to 9
- keys: bfloat16 [16384, 256], P(('grp', 'dev')), may hold values from -6 to 6
- values: bfloat16 [16384, 256], P(('grp', 'dev')), may hold values from -18 to 18
- prefix_keys: bfloat16 [32, 1024, 256], P('grp', 'dev'), may hold values from -6 to 6
- cached_prefix_values: bfloat16 [32, 1024, 256], P('grp', 'dev'), may hold values from -18 to 18
- out_weight: bfloat16 [1024, 2048], replicated, may hold values from -0.1875 to 0.1875
- norm_gain: float32 [2048], replicated, may hold values from 0.25 to 1.75
- w_gate: bfloat16 [2048, 8192], P('grp', 'dev'), may hold values from -0.125 to 0.125
- w_up: bfloat16 [2048, 8192], P('grp', 'dev'), may hold values from -0.125 to 0.125
- w_down: bfloat16 [8192, 2048], P('dev', 'grp'), may hold values from -0.0625 to 0.0625
- suffix_lengths: int32 [8, 32], P('grp'), may hold values from 1 to 128, 2048 in all within a row
- request_group: int32 [8, 32], P('grp'), may hold values from 0 to 3, as said below
- placement_order: int32 [8, 32], P('grp'), may hold values from 0 to 31, each once within a row
Outputs:
- layer_out: bfloat16 [16384, 2048], P(('grp', 'dev'))
Inputs may be any that keep to these rules, and one draw needn't show every extreme that they name: `suffix_lengths`: the 32 lengths of one row sum to 2048. `request_group`: each row names each of its 4 groups exactly 8 times. `placement_order`: each row is an ordering of its 32 requests.
All inputs are finite; a program needn't handle non-finite values.
Results may differ from a plain program's by a relative error of at most 0.012.
Values may be sent and summed in bfloat16 or wider, within the bound.
A program may use at most 128 MiB of HBM per device.

v0:
```python
import math
import jax
import jax.numpy as jnp
from jax import lax
from jax.sharding import PartitionSpec as P

HEAD_SIZE = 64
NEG_FILL = -1e30
EPSILON = 1e-05


def row_layout(lengths, group_map, packed_order):
    request_count = lengths.shape[0]
    picked = (packed_order[:, None] == jnp.arange(request_count, dtype=jnp.int32)[None, :]).astype(
        jnp.int32
    )
    packed_len = jnp.sum(picked * lengths[None, :], axis=1)
    packed_group = jnp.sum(picked * group_map[None, :], axis=1)
    ends_at = jnp.cumsum(packed_len)
    return (ends_at - packed_len, ends_at, packed_group)


def token_info(token_rows, starts_at, ends_at, packed_group):
    inside = (
        (token_rows[:, None] >= starts_at[None, :]) & (token_rows[:, None] < ends_at[None, :])
    ).astype(jnp.int32)
    return (
        jnp.sum(inside * packed_group[None, :], axis=1),
        jnp.sum(inside * starts_at[None, :], axis=1),
    )


def block_partial(rows_of_queries, allowed, rows_of_keys, rows_of_values):
    query_row_count = rows_of_queries.shape[0]
    key_row_count = rows_of_keys.shape[0]
    heads_kv = rows_of_keys.shape[1] // HEAD_SIZE
    heads_of_queries = rows_of_queries.reshape(query_row_count, heads_kv, -1, HEAD_SIZE)
    heads_of_keys = rows_of_keys.reshape(key_row_count, heads_kv, HEAD_SIZE)
    heads_of_values = rows_of_values.reshape(key_row_count, heads_kv, HEAD_SIZE)
    scores = jnp.einsum(
        "nkrd,mkd->nkrm", heads_of_queries, heads_of_keys, preferred_element_type=jnp.float32
    ) * HEAD_SIZE ** (-0.5)
    scores = jnp.where(allowed[:, None, None, :], scores, NEG_FILL)
    maxima = jnp.max(scores, axis=-1)
    weights = jnp.exp(scores - maxima[..., None])
    totals = jnp.sum(weights, axis=-1)
    numerator = jnp.einsum(
        "nkrm,mkd->nkrd",
        weights.astype(jnp.bfloat16),
        heads_of_values,
        preferred_element_type=jnp.float32,
    )
    return (numerator / totals[..., None], maxima, totals)


def merge_all(local_output, local_maximum, local_sum, block_outs, block_maxima, block_sums):
    highest = jnp.maximum(local_maximum, jnp.max(block_maxima, axis=0))
    own_scale = local_sum * jnp.exp(local_maximum - highest)
    scales = block_sums * jnp.exp(block_maxima - highest[None])
    numerator = own_scale[..., None] * local_output + jnp.sum(
        scales[..., None] * block_outs.astype(jnp.float32), axis=0
    )
    return numerator / (own_scale + jnp.sum(scales, axis=0))[..., None]


def shards(
    residual,
    queries,
    keys,
    values,
    prefix_keys,
    cached_prefix_values,
    out_weight,
    norm_gain,
    w_gate,
    w_up,
    w_down,
    suffix_lengths,
    request_group,
    placement_order,
):
    tok_rows = queries.shape[0]
    key_value_width = keys.shape[1]
    span = prefix_keys.shape[1]
    block_keys = prefix_keys.shape[0] * span
    starts_at, ends_at, packed_group = row_layout(
        suffix_lengths[0], request_group[0], placement_order[0]
    )
    base_row = lax.axis_index("dev") * tok_rows
    own_rows = base_row + jnp.arange(tok_rows, dtype=jnp.int32)
    own_group, own_start = token_info(own_rows, starts_at, ends_at, packed_group)
    window = base_row - tok_rows + jnp.arange(2 * tok_rows, dtype=jnp.int32)
    suffix_mask = (window[None, :] >= own_start[:, None]) & (window[None, :] <= own_rows[:, None])
    key_group = jnp.arange(block_keys, dtype=jnp.int32) // span
    row_queries, row_keys, row_values = (
        lax.all_gather(queries, "dev", axis=0, tiled=True),
        lax.all_gather(keys, "dev", axis=0, tiled=True),
        lax.all_gather(values, "dev", axis=0, tiled=True),
    )
    prior_row = jnp.maximum(base_row - tok_rows, 0)
    before_keys = lax.dynamic_slice_in_dim(row_keys, prior_row, tok_rows, 0)
    before_values = lax.dynamic_slice_in_dim(row_values, prior_row, tok_rows, 0)
    local_output, local_maximum, local_sum = block_partial(
        queries,
        suffix_mask,
        jnp.concatenate([before_keys, keys], axis=0),
        jnp.concatenate([before_values, values], axis=0),
    )
    flat_keys = prefix_keys.reshape(block_keys, key_value_width)
    flat_values = cached_prefix_values.reshape(block_keys, key_value_width)
    row_count = row_queries.shape[0]
    row_group = token_info(
        jnp.arange(row_count, dtype=jnp.int32), starts_at, ends_at, packed_group
    )[0]
    step_rows = math.gcd(row_count, 512)

    def owner_block(block_index):
        first_row = block_index * step_rows
        rows_of_queries = lax.dynamic_slice_in_dim(row_queries, first_row, step_rows, 0)
        group_rows = lax.dynamic_slice_in_dim(row_group, first_row, step_rows, 0)
        allowed = group_rows[:, None] == key_group[None, :]
        part_out, maxima, totals = block_partial(rows_of_queries, allowed, flat_keys, flat_values)
        return (
            part_out.astype(jnp.bfloat16).reshape(step_rows, -1),
            maxima.reshape(step_rows, -1),
            totals.reshape(step_rows, -1),
        )

    part_outs, part_maxima, part_sums = lax.map(
        owner_block, jnp.arange(row_count // step_rows, dtype=jnp.int32)
    )
    peers = row_count // tok_rows
    part_outs = part_outs.reshape(peers, tok_rows, -1)
    part_maxima = part_maxima.reshape(peers, tok_rows, -1)
    part_sums = part_sums.reshape(peers, tok_rows, -1)
    back_outs = lax.all_to_all(part_outs, "dev", split_axis=0, concat_axis=0, tiled=True)
    back_maxima, back_sums = (
        lax.all_to_all(part_maxima, "dev", split_axis=0, concat_axis=0, tiled=True),
        lax.all_to_all(part_sums, "dev", split_axis=0, concat_axis=0, tiled=True),
    )
    merged = merge_all(
        local_output,
        local_maximum,
        local_sum,
        back_outs.reshape((peers,) + local_output.shape),
        back_maxima.reshape((peers,) + local_maximum.shape),
        back_sums.reshape((peers,) + local_sum.shape),
    )
    attention = merged.astype(jnp.bfloat16).reshape(tok_rows, -1)
    hidden_state = residual.astype(jnp.float32) + jnp.dot(
        attention, out_weight, preferred_element_type=jnp.float32
    )
    normed = (
        hidden_state
        * lax.rsqrt(jnp.mean(hidden_state * hidden_state, axis=-1, keepdims=True) + EPSILON)
        * norm_gain
    ).astype(jnp.bfloat16)
    full_gate, full_up, full_down = (
        lax.all_gather(w_gate, "grp", axis=0, tiled=True),
        lax.all_gather(w_up, "grp", axis=0, tiled=True),
        lax.all_gather(w_down, "grp", axis=1, tiled=True),
    )
    shard_piece = lax.all_gather(normed, "dev", axis=0, tiled=True)
    gate_value = jnp.dot(shard_piece, full_gate, preferred_element_type=jnp.float32)
    up_value = jnp.dot(shard_piece, full_up, preferred_element_type=jnp.float32)
    activation = (jax.nn.silu(gate_value) * up_value).astype(jnp.bfloat16)
    mlp_sum = lax.psum_scatter(
        jnp.dot(activation, full_down, preferred_element_type=jnp.float32).astype(jnp.bfloat16),
        "dev",
        scatter_dimension=0,
        tiled=True,
    ).astype(jnp.float32)
    return (hidden_state + mlp_sum).astype(jnp.bfloat16)


def solution(mesh):
    placed = (
        P(("grp", "dev"), None),
        P(("grp", "dev"), None),
        P(("grp", "dev"), None),
        P(("grp", "dev"), None),
        P("grp", "dev", None),
        P("grp", "dev", None),
        P(),
        P(),
        P("grp", "dev"),
        P("grp", "dev"),
        P("dev", "grp"),
        P("grp", None),
        P("grp", None),
        P("grp", None),
    )
    return jax.shard_map(
        shards, mesh=mesh, in_specs=placed, out_specs=P(("grp", "dev"), None), check_vma=False
    )
```

profile of v0, /device:TPU:0, one launch (start us, length us, event | category | flops | bytes accessed | tf_op | source)
XLA Modules:
  0.0 460.7 jit_solution(9504915503423663527)
XLA Ops:
  6.5 1.8 copy.63
  11.2 57.8 %all-gather.10.cloned.1.call-done = bf16[2048,1024]{0,1:T(8,128)(2,1)} async-done(((bf16[128,1024]{0,1:T(8,128)(2,1)}), bf16[2048,1024]{0,1:T(8,128)(2,1)}) %all-gather.10.cloned.1.call-update) | async-done | bytes 4194320 | tf_op jit(solution)/shard_map/all_gather | solution.py:96
  69.0 64.9 %while.15 = (s32[]{:T(128)}, bf16[4,512,1024]{2,1,0:T(8,128)(2,1)}, f32[4,512,16]{1,0,2:T(4,128)S(1)}, f32[4,512,16]{1,0,2:T(4,128)S(1)}, s32[4]{0:T(128)S(1)}, ...) while((s32[]{:T(128)}, bf16[4,512,1024]{2,1,0:T(8,128)(2,1)}, ...), condition=%wide.region_10.11_spmd.clone, body=%wide.region_7.10_spmd.clone.sunk | while | flops 561104896 | bytes 69378800 | solution.py:129
  74.1 1.8 fusion.50
  75.9 1.4 copy-done
  77.5 5.6 %fusion.51 = bf16[512,4,4,64]{0,3,2,1:T(8,128)(2,1)S(1)} fusion(f32[4,512,4,256]{1,3,2,0:T(8,128)} %copy-done, f32[512,4,4]{0,2,1:T(4,128)S(1)} %get-tuple-element.183, pred[512,256]{0,1:T(8,128)(4,1)S(1)} %broadcast_compare_fusion.2, f32[512,4,4]{0,2,1:T(4,128)S(1)} %fusion.50, bf16[256,4,64,1]{2,1,0,3:T(4,128)(2,1)S(1)} %bitcast.111), kind=kOutput, calls=%fused_computation.10.clone.1 | convolution fusion | flops 277872640 | bytes 9764864 | tf_op jit(solution)/shard_map/while/body/eval_jaxpr/nkrm,mkd->nkrd/dot_general | solution.py:47
  89.0 1.4 bitcast_reduce_fusion.2
  90.4 1.8 fusion.50
  92.2 1.4 copy-done
  93.8 5.6 %fusion.51 = bf16[512,4,4,64]{0,3,2,1:T(8,128)(2,1)S(1)} fusion(f32[4,512,4,256]{1,3,2,0:T(8,128)} %copy-done, f32[512,4,4]{0,2,1:T(4,128)S(1)} %get-tuple-element.183, pred[512,256]{0,1:T(8,128)(4,1)S(1)} %broadcast_compare_fusion.2, f32[512,4,4]{0,2,1:T(4,128)S(1)} %fusion.50, bf16[256,4,64,1]{2,1,0,3:T(4,128)(2,1)S(1)} %bitcast.111), kind=kOutput, calls=%fused_computation.10.clone.1 | convolution fusion | flops 277872640 | bytes 9764864 | tf_op jit(solution)/shard_map/while/body/eval_jaxpr/nkrm,mkd->nkrd/dot_general | solution.py:47
  105.2 1.4 bitcast_reduce_fusion.2
  106.6 1.8 fusion.50
  108.4 1.4 copy-done
  110.0 5.6 %fusion.51 = bf16[512,4,4,64]{0,3,2,1:T(8,128)(2,1)S(1)} fusion(f32[4,512,4,256]{1,3,2,0:T(8,128)} %copy-done, f32[512,4,4]{0,2,1:T(4,128)S(1)} %get-tuple-element.183, pred[512,256]{0,1:T(8,128)(4,1)S(1)} %broadcast_compare_fusion.2, f32[512,4,4]{0,2,1:T(4,128)S(1)} %fusion.50, bf16[256,4,64,1]{2,1,0,3:T(4,128)(2,1)S(1)} %bitcast.111), kind=kOutput, calls=%fused_computation.10.clone.1 | convolution fusion | flops 277872640 | bytes 9764864 | tf_op jit(solution)/shard_map/while/body/eval_jaxpr/nkrm,mkd->nkrd/dot_general | solution.py:47
  122.9 1.8 fusion.50
  124.6 1.4 copy-done
  126.2 5.6 %fusion.51 = bf16[512,4,4,64]{0,3,2,1:T(8,128)(2,1)S(1)} fusion(f32[4,512,4,256]{1,3,2,0:T(8,128)} %copy-done, f32[512,4,4]{0,2,1:T(4,128)S(1)} %get-tuple-element.183, pred[512,256]{0,1:T(8,128)(4,1)S(1)} %broadcast_compare_fusion.2, f32[512,4,4]{0,2,1:T(4,128)S(1)} %fusion.50, bf16[256,4,64,1]{2,1,0,3:T(4,128)(2,1)S(1)} %bitcast.111), kind=kOutput, calls=%fused_computation.10.clone.1 | convolution fusion | flops 277872640 | bytes 9764864 | tf_op jit(solution)/shard_map/while/body/eval_jaxpr/nkrm,mkd->nkrd/dot_general | solution.py:47
  134.6 4.9 %all-to-all-start = ((f32[16,128,16]{1,2,0:T(8,128)}), f32[16,128,16]{1,2,0:T(8,128)S(1)}, u32[]{:S(2)}, u32[]{:S(2)}) async-start(f32[16,128,16]{1,2,0:T(8,128)} %copy.66), calls=%async_computation | async-start | bytes 262144 | tf_op jit(solution)/shard_map/all_to_all | solution.py:138
  140.3 7.2 %all-to-all-done = f32[16,128,16]{1,2,0:T(8,128)S(1)} async-done(((f32[16,128,16]{1,2,0:T(8,128)}), f32[16,128,16]{1,2,0:T(8,128)S(1)}, u32[]{:S(2)}, u32[]{:S(2)}) %all-to-all-start) | async-done | bytes 131104 | tf_op jit(solution)/shard_map/all_to_all | solution.py:138
  147.6 3.5 all-to-all-start.1
  151.1 6.4 %copy.75 = bf16[16,128,1024]{1,2,0:T(8,128)(2,1)} copy(bf16[16,128,1024]{2,1,0:T(8,128)(2,1)} %bitcast.112) | data formatting | bytes 8388608 | tf_op jit(solution)/shard_map/reshape | solution.py:133
  157.5 1.9 all-to-all-done.1
  159.4 5.4 %all-to-all-start.2 = ((bf16[16,128,1024]{1,2,0:T(8,128)(2,1)}), bf16[16,128,1024]{1,2,0:T(8,128)(2,1)}, u32[]{:S(2)}, u32[]{:S(2)}) async-start(bf16[16,128,1024]{1,2,0:T(8,128)(2,1)} %copy.75), calls=%async_computation.2 | async-start | bytes 8388608 | tf_op jit(solution)/shard_map/all_to_all | solution.py:136
  168.3 50.7 %all-to-all-done.2 = bf16[16,128,1024]{1,2,0:T(8,128)(2,1)} async-done(((bf16[16,128,1024]{1,2,0:T(8,128)(2,1)}), bf16[16,128,1024]{1,2,0:T(8,128)(2,1)}, u32[]{:S(2)}, u32[]{:S(2)}) %all-to-all-start.2) | async-done | bytes 4194336 | tf_op jit(solution)/shard_map/all_to_all | solution.py:136
  219.0 3.2 fusion.16
  226.0 68.2 %all-gather.14.cloned.1.call-done = bf16[2048,2048]{1,0:T(8,128)(2,1)} async-done(((bf16[128,2048]{1,0:T(8,128)(2,1)}), bf16[2048,2048]{1,0:T(8,128)(2,1)}) %all-gather.14.cloned.1.call-update) | async-done | bytes 8388624 | tf_op jit(solution)/shard_map/all_gather | solution.py:163
  294.2 10.4 %fusion.30 = f32[2048,512]{1,0:T(8,128)} fusion(bf16[2048,2048]{1,0:T(8,128)(2,1)} %all-gather.14.cloned.1.call-done, bf16[2048,512]{1,0:T(8,128)(2,1)} %all-gather.16.cloned.1.call-done), kind=kOutput, calls=%fused_computation.64 | convolution fusion | flops 4294967296 | bytes 14680064 | tf_op jit(solution)/shard_map/dot_general | solution.py:164
  304.6 16.0 %all-gather.18.cloned.1.call-done = bf16[2048,512]{1,0:T(8,128)(2,1)} async-done(((bf16[256,512]{1,0:T(8,128)(2,1)}), bf16[2048,512]{1,0:T(8,128)(2,1)}) %all-gather.18.cloned.1.call-update) | async-done | bytes 2097168 | tf_op jit(solution)/shard_map/all_gather | solution.py:160
  320.6 28.9 %all-gather.20.cloned.1.call-done = bf16[512,2048]{1,0:T(8,128)(2,1)} async-done(((bf16[512,256]{1,0:T(8,128)(2,1)}), bf16[512,2048]{1,0:T(8,128)(2,1)}) %all-gather.20.cloned.1.call-update) | async-done | bytes 2097168 | tf_op jit(solution)/shard_map/all_gather | solution.py:161
  349.5 15.2 %convolution_convert_fusion = bf16[2048,2048]{1,0:T(8,128)(2,1)} fusion(bf16[512,2048]{1,0:T(8,128)(2,1)} %all-gather.20.cloned.1.call-done, f32[2048,512]{1,0:T(8,128)} %fusion.30, bf16[2048,2048]{1,0:T(8,128)(2,1)} %all-gather.14.cloned.1.call-done, bf16[2048,512]{1,0:T(8,128)(2,1)} %all-gather.18.cloned.1.call-done), kind=kOutput, calls=%fused_computation.25 | convolution fusion | flops 8600420352 | bytes 25165824 | tf_op jit(solution)/shard_map/dot_general | solution.py:168
  364.8 87.2 %reduce-scatter.2.cloned.1.call-done = bf16[128,2048]{1,0:T(8,128)(2,1)} async-done(((bf16[2048,2048]{1,0:T(8,128)(2,1)}), bf16[128,2048]{1,0:T(8,128)(2,1)}) %reduce-scatter.2.cloned.1.call-update) | async-done | bytes 524304 | tf_op jit(solution)/shard_map/reduce_scatter | solution.py:167
  451.9 1.9 add_convert_fusion
  (134 shorter events, 35.6 us)
Async XLA Ops:
  6.5 62.4 %all-gather.10.cloned.1.call-start = ((), (), s32[]{:S(2)}) async-start(), calls=%async_computation.5 | async-start | bytes 4456448 | tf_op jit(solution)/shard_map/all_gather | solution.py:96
  8.4 157.6 %all-gather.12.cloned.1.call-start = ((), (), s32[]{:S(2)}) async-start(), calls=%async_computation.6 | async-start | bytes 1114112 | tf_op jit(solution)/shard_map/all_gather | solution.py:98
  9.1 156.8 %all-gather.8.cloned.1.call-start = ((), (), s32[]{:S(2)}) async-start(), calls=%async_computation.4 | async-start | bytes 1114112 | tf_op jit(solution)/shard_map/all_gather | solution.py:97
  74.1 3.2 copy-start
  74.1 3.2 copy-start.2
  90.4 3.2 copy-start
  90.4 3.2 copy-start.2
  106.6 3.2 copy-start
  106.6 3.2 copy-start.2
  122.8 3.2 copy-start
  122.9 3.2 copy-start.2
  134.6 12.9 %all-to-all-start = ((f32[16,128,16]{1,2,0:T(8,128)}), f32[16,128,16]{1,2,0:T(8,128)S(1)}, u32[]{:S(2)}, u32[]{:S(2)}) async-start(f32[16,128,16]{1,2,0:T(8,128)} %copy.66), calls=%async_computation | async-start | bytes 262144 | tf_op jit(solution)/shard_map/all_to_all | solution.py:138
  147.6 11.8 %all-to-all-start.1 = ((f32[16,128,16]{1,2,0:T(8,128)}), f32[16,128,16]{1,2,0:T(8,128)S(1)}, u32[]{:S(2)}, u32[]{:S(2)}) async-start(f32[16,128,16]{1,2,0:T(8,128)} %copy.70), calls=%async_computation.1 | async-start | bytes 262144 | tf_op jit(solution)/shard_map/all_to_all | solution.py:139
  157.5 9.4 %copy-start.5 = (bf16[128,256]{1,0:T(8,128)(2,1)S(1)}, bf16[128,256]{1,0:T(8,128)(2,1)}, u32[]{:S(2)}) copy-start(bf16[128,256]{1,0:T(8,128)(2,1)} %param.18) | copy-start | bytes 196612
  157.5 9.5 %copy-start.6 = (bf16[128,256]{1,0:T(8,128)(2,1)S(1)}, bf16[128,256]{1,0:T(8,128)(2,1)}, u32[]{:S(2)}) copy-start(bf16[128,256]{1,0:T(8,128)(2,1)} %param.19) | copy-start | bytes 196612
  157.5 9.7 %copy-start.3 = (bf16[128,1024]{0,1:T(8,128)(2,1)S(1)}, bf16[128,1024]{0,1:T(8,128)(2,1)}, u32[]{:S(2)}) copy-start(bf16[128,1024]{0,1:T(8,128)(2,1)} %copy.63) | copy-start | bytes 786436
  159.4 59.6 %all-to-all-start.2 = ((bf16[16,128,1024]{1,2,0:T(8,128)(2,1)}), bf16[16,128,1024]{1,2,0:T(8,128)(2,1)}, u32[]{:S(2)}, u32[]{:S(2)}) async-start(bf16[16,128,1024]{1,2,0:T(8,128)(2,1)} %copy.75), calls=%async_computation.2 | async-start | bytes 8388608 | tf_op jit(solution)/shard_map/all_to_all | solution.py:136
  164.9 61.1 %all-gather.16.cloned.1.call-start = ((), (), s32[]{:S(2)}) async-start(), calls=%async_computation.8 | async-start | bytes 2359296 | tf_op jit(solution)/shard_map/all_gather | solution.py:159
  165.4 128.8 %all-gather.14.cloned.1.call-start = ((), (), s32[]{:S(2)}) async-start(), calls=%async_computation.7 | async-start | bytes 8912896 | tf_op jit(solution)/shard_map/all_gather | solution.py:163
  168.3 54.4 %copy-start.4 = (bf16[128,2048]{1,0:T(8,128)(2,1)S(1)}, bf16[128,2048]{1,0:T(8,128)(2,1)}, u32[]{:S(2)}) copy-start(bf16[128,2048]{1,0:T(8,128)(2,1)} %param.16) | copy-start | bytes 1572868
  219.0 3.7 copy-start.1
  222.7 0.9 copy-start.7
  224.6 96.1 %all-gather.18.cloned.1.call-start = ((), (), s32[]{:S(2)}) async-start(), calls=%async_computation.9 | async-start | bytes 2359296 | tf_op jit(solution)/shard_map/all_gather | solution.py:160
  225.2 124.3 %all-gather.20.cloned.1.call-start = ((), (), s32[]{:S(2)}) async-start(), calls=%async_computation.10 | async-start | bytes 2359296 | tf_op jit(solution)/shard_map/all_gather | solution.py:161
  225.9 226.0 %reduce-scatter.2.cloned.1.call-start = ((), (), s32[]{:S(2)}) async-start(), calls=%async_computation.11 | async-start | bytes 8912896 | tf_op jit(solution)/shard_map/reduce_scatter | solution.py:167
Sparse Core Ops, SparseCore 0:
  9.4 59.4 all-gather.9
  71.1 41.8 all-gather.11
  115.2 42.2 all-gather.7
  167.1 26.6 all-gather.15
  224.7 69.4 all-gather.13
  295.8 24.8 all-gather.17
  322.3 27.1 all-gather.19
  364.9 87.0 reduce-scatter.1
where the time goes:
time: 462 us; the launch traced here: 461 us
  waiting for transfers between devices  321 us (69%)
  matrix products  55.4 us (12%)
  local copies, waits for them, and re-layouts  37.8 us (8%)
  other arithmetic  15.6 us (3%)
  starting transfers between devices  14.3 us (3%)
  between operations  13.8 us (3%)
    reduce_scatter x1, waiting for transfers between devices, shards(): lax.psum_scatter(jnp.dot(activation, full_down, preferred_element_type=jn...  87.2 us
    all_gather x1, waiting for transfers between devices, shards(): shard_piece = lax.all_gather(normed, 'dev', axis=0, tiled=True)  68.2 us
    all_gather x1, waiting for transfers between devices, shards(): lax.all_gather(queries, 'dev', axis=0, tiled=True)  57.8 us
    all_to_all x1, waiting for transfers between devices, shards(): lax.all_to_all(part_outs, 'dev', split_axis=0, concat_axis=0, tiled=True)  50.7 us
    all_gather x1, waiting for transfers between devices, shards(): lax.all_gather(w_down, 'grp', axis=1, tiled=True)  28.9 us
    dot_general x5, matrix products, block_partial(): jnp.einsum('nkrm,mkd->nkrd', weights.astype(jnp.bfloat16), heads_of_value...  22.8 us
    all_gather x1, waiting for transfers between devices, shards(): lax.all_gather(w_up, 'grp', axis=0, tiled=True)  16 us
    dot_general x1, matrix products, shards(): jnp.dot(activation, full_down, preferred_element_type=jnp.float32)  15.2 us
  transfers between devices with their start and end apart: 11, of which 8 were waited for; matrix products, arithmetic and copies ran while one was open for 18% of the time, Pallas kernels for 0%

commit v1 on v0

--- a/solution.py
+++ b/solution.py
@@ -157,7 +157,9 @@
     ).astype(jnp.bfloat16)
     full_gate, full_up, full_down = (
         lax.all_gather(w_gate, "grp", axis=0, tiled=True),
-        lax.all_gather(w_up, "grp", axis=0, tiled=True),
+        jnp.concatenate(
+            lax.all_to_all(jnp.stack([w_up] * lax.axis_size("grp")), "grp", 0, 0), axis=0
+        ),
         lax.all_gather(w_down, "grp", axis=1, tiled=True),
     )
     shard_piece = lax.all_gather(normed, "dev", axis=0, tiled=True)

time: 462 us -> 434 us (0.939)
  waiting for transfers between devices: 321 us -> 288 us
    all_gather x1 -> x0, waiting for transfers between devices: 16 us -> none  [shards(): lax.all_gather(w_up, 'grp', axis=0, tiled=True)]
    all_gather x1, waiting for transfers between devices: 28.9 us -> 17.4 us  [shards(): lax.all_gather(w_down, 'grp', axis=1, tiled=True)]
    all_gather x1, waiting for transfers between devices: 68.2 us -> 63.2 us  [shards(): shard_piece = lax.all_gather(normed, 'dev', axis=0, tiled=True)]
  transfers between devices with their start and end apart: 11 -> 11, of which waited for: 8 -> 7; matrix products, arithmetic and copies ran while one was open for 18% -> 20% of each run, Pallas kernels for 0% -> 0%
where the time goes in v1:
time: 434 us; the launch traced here: 433 us
  waiting for transfers between devices  288 us (66%)
  matrix products  54.8 us (13%)
  local copies, waits for them, and re-layouts  39.3 us (9%)
  starting transfers between devices  18.6 us (4%)
  other arithmetic  15.6 us (4%)
  between operations  13.8 us (3%)
    reduce_scatter x1, waiting for transfers between devices, shards(): lax.psum_scatter(jnp.dot(activation, full_down, preferred_element_type=jn...  87 us
    all_gather x1, waiting for transfers between devices, shards(): shard_piece = lax.all_gather(normed, 'dev', axis=0, tiled=True)  63.2 us
    all_gather x1, waiting for transfers between devices, shards(): lax.all_gather(queries, 'dev', axis=0, tiled=True)  57.8 us
    all_to_all x1, waiting for transfers between devices, shards(): lax.all_to_all(part_outs, 'dev', split_axis=0, concat_axis=0, tiled=True)  50.7 us
    dot_general x5, matrix products, block_partial(): jnp.einsum('nkrm,mkd->nkrd', weights.astype(jnp.bfloat16), heads_of_value...  22.8 us
    all_gather x1, waiting for transfers between devices, shards(): lax.all_gather(w_down, 'grp', axis=1, tiled=True)  17.4 us
    dot_general x1, matrix products, shards(): jnp.dot(activation, full_down, preferred_element_type=jnp.float32)  14.7 us
    dot_general x1, matrix products, shards(): jnp.dot(shard_piece, full_gate, preferred_element_type=jnp.float32)  10.4 us
  transfers between devices with their start and end apart: 11, of which 7 were waited for; matrix products, arithmetic and copies ran while one was open for 20% of the time, Pallas kernels for 0%

profile of v1, /device:TPU:0, one launch (start us, length us, event | category | flops | bytes accessed | tf_op | source)
XLA Modules:
  0.0 432.5 jit_solution(21062000987882008)
XLA Ops:
  6.5 1.8 copy.63
  11.2 57.8 %all-gather.9.cloned.1.call-done = bf16[2048,1024]{0,1:T(8,128)(2,1)} async-done(((bf16[128,1024]{0,1:T(8,128)(2,1)}), bf16[2048,1024]{0,1:T(8,128)(2,1)}) %all-gather.9.cloned.1.call-update) | async-done | bytes 4194320 | tf_op jit(solution)/shard_map/all_gather | solution.py:96
  69.0 64.9 %while.15 = (s32[]{:T(128)}, bf16[4,512,1024]{2,1,0:T(8,128)(2,1)}, f32[4,512,16]{1,0,2:T(4,128)S(1)}, f32[4,512,16]{1,0,2:T(4,128)S(1)}, s32[4]{0:T(128)S(1)}, ...) while((s32[]{:T(128)}, bf16[4,512,1024]{2,1,0:T(8,128)(2,1)}, ...), condition=%wide.region_10.11_spmd.clone, body=%wide.region_7.10_spmd.clone.sunk | while | flops 561104896 | bytes 69378800 | solution.py:129
  74.1 1.8 fusion.50
  75.9 1.4 copy-done
  77.5 5.6 %fusion.51 = bf16[512,4,4,64]{0,3,2,1:T(8,128)(2,1)S(1)} fusion(f32[4,512,4,256]{1,3,2,0:T(8,128)} %copy-done, f32[512,4,4]{0,2,1:T(4,128)S(1)} %get-tuple-element.183, pred[512,256]{0,1:T(8,128)(4,1)S(1)} %broadcast_compare_fusion.2, f32[512,4,4]{0,2,1:T(4,128)S(1)} %fusion.50, bf16[256,4,64,1]{2,1,0,3:T(4,128)(2,1)S(1)} %bitcast.112), kind=kOutput, calls=%fused_computation.10.clone.1 | convolution fusion | flops 277872640 | bytes 9764864 | tf_op jit(solution)/shard_map/while/body/eval_jaxpr/nkrm,mkd->nkrd/dot_general | solution.py:47
  89.0 1.4 bitcast_reduce_fusion.2
  90.4 1.8 fusion.50
  92.2 1.4 copy-done
  93.8 5.6 %fusion.51 = bf16[512,4,4,64]{0,3,2,1:T(8,128)(2,1)S(1)} fusion(f32[4,512,4,256]{1,3,2,0:T(8,128)} %copy-done, f32[512,4,4]{0,2,1:T(4,128)S(1)} %get-tuple-element.183, pred[512,256]{0,1:T(8,128)(4,1)S(1)} %broadcast_compare_fusion.2, f32[512,4,4]{0,2,1:T(4,128)S(1)} %fusion.50, bf16[256,4,64,1]{2,1,0,3:T(4,128)(2,1)S(1)} %bitcast.112), kind=kOutput, calls=%fused_computation.10.clone.1 | convolution fusion | flops 277872640 | bytes 9764864 | tf_op jit(solution)/shard_map/while/body/eval_jaxpr/nkrm,mkd->nkrd/dot_general | solution.py:47
  106.6 1.8 fusion.50
  108.4 1.4 copy-done
  110.0 5.6 %fusion.51 = bf16[512,4,4,64]{0,3,2,1:T(8,128)(2,1)S(1)} fusion(f32[4,512,4,256]{1,3,2,0:T(8,128)} %copy-done, f32[512,4,4]{0,2,1:T(4,128)S(1)} %get-tuple-element.183, pred[512,256]{0,1:T(8,128)(4,1)S(1)} %broadcast_compare_fusion.2, f32[512,4,4]{0,2,1:T(4,128)S(1)} %fusion.50, bf16[256,4,64,1]{2,1,0,3:T(4,128)(2,1)S(1)} %bitcast.112), kind=kOutput, calls=%fused_computation.10.clone.1 | convolution fusion | flops 277872640 | bytes 9764864 | tf_op jit(solution)/shard_map/while/body/eval_jaxpr/nkrm,mkd->nkrd/dot_general | solution.py:47
  122.9 1.8 fusion.50
  124.6 1.4 copy-done
  126.2 5.6 %fusion.51 = bf16[512,4,4,64]{0,3,2,1:T(8,128)(2,1)S(1)} fusion(f32[4,512,4,256]{1,3,2,0:T(8,128)} %copy-done, f32[512,4,4]{0,2,1:T(4,128)S(1)} %get-tuple-element.183, pred[512,256]{0,1:T(8,128)(4,1)S(1)} %broadcast_compare_fusion.2, f32[512,4,4]{0,2,1:T(4,128)S(1)} %fusion.50, bf16[256,4,64,1]{2,1,0,3:T(4,128)(2,1)S(1)} %bitcast.112), kind=kOutput, calls=%fused_computation.10.clone.1 | convolution fusion | flops 277872640 | bytes 9764864 | tf_op jit(solution)/shard_map/while/body/eval_jaxpr/nkrm,mkd->nkrd/dot_general | solution.py:47
  134.6 4.9 %all-to-all-start = ((f32[16,128,16]{1,2,0:T(8,128)}), f32[16,128,16]{1,2,0:T(8,128)S(1)}, u32[]{:S(2)}, u32[]{:S(2)}) async-start(f32[16,128,16]{1,2,0:T(8,128)} %copy.66), calls=%async_computation | async-start | bytes 262144 | tf_op jit(solution)/shard_map/all_to_all | solution.py:138
  140.3 7.2 %all-to-all-done = f32[16,128,16]{1,2,0:T(8,128)S(1)} async-done(((f32[16,128,16]{1,2,0:T(8,128)}), f32[16,128,16]{1,2,0:T(8,128)S(1)}, u32[]{:S(2)}, u32[]{:S(2)}) %all-to-all-start) | async-done | bytes 131104 | tf_op jit(solution)/shard_map/all_to_all | solution.py:138
  147.6 3.5 all-to-all-start.1
  151.1 6.4 %copy.75 = bf16[16,128,1024]{1,2,0:T(8,128)(2,1)} copy(bf16[16,128,1024]{2,1,0:T(8,128)(2,1)} %bitcast.113) | data formatting | bytes 8388608 | tf_op jit(solution)/shard_map/reshape | solution.py:133
  157.5 1.9 all-to-all-done.1
  159.4 5.4 %all-to-all-start.2 = ((bf16[16,128,1024]{1,2,0:T(8,128)(2,1)}), bf16[16,128,1024]{1,2,0:T(8,128)(2,1)}, u32[]{:S(2)}, u32[]{:S(2)}) async-start(bf16[16,128,1024]{1,2,0:T(8,128)(2,1)} %copy.75), calls=%async_computation.2 | async-start | bytes 8388608 | tf_op jit(solution)/shard_map/all_to_all | solution.py:136
  168.3 50.7 %all-to-all-done.2 = bf16[16,128,1024]{1,2,0:T(8,128)(2,1)} async-done(((bf16[16,128,1024]{1,2,0:T(8,128)(2,1)}), bf16[16,128,1024]{1,2,0:T(8,128)(2,1)}, u32[]{:S(2)}, u32[]{:S(2)}) %all-to-all-start.2) | async-done | bytes 4194336 | tf_op jit(solution)/shard_map/all_to_all | solution.py:136
  219.0 3.2 fusion.16
  225.2 1.5 stack.2
  226.7 4.3 all-to-all-start.3
  231.0 63.2 %all-gather.13.cloned.1.call-done = bf16[2048,2048]{1,0:T(8,128)(2,1)} async-done(((bf16[128,2048]{1,0:T(8,128)(2,1)}), bf16[2048,2048]{1,0:T(8,128)(2,1)}) %all-gather.13.cloned.1.call-update) | async-done | bytes 8388624 | tf_op jit(solution)/shard_map/all_gather | solution.py:165
  294.2 10.4 %fusion.30 = f32[2048,512]{1,0:T(8,128)} fusion(bf16[2048,2048]{1,0:T(8,128)(2,1)} %all-gather.13.cloned.1.call-done, bf16[2048,512]{1,0:T(8,128)(2,1)} %all-gather.15.cloned.1.call-done), kind=kOutput, calls=%fused_computation.64 | convolution fusion | flops 4294967296 | bytes 14680064 | tf_op jit(solution)/shard_map/dot_general | solution.py:166
  304.7 17.4 %all-gather.17.cloned.1.call-done = bf16[512,2048]{1,0:T(8,128)(2,1)} async-done(((bf16[512,256]{1,0:T(8,128)(2,1)}), bf16[512,2048]{1,0:T(8,128)(2,1)}) %all-gather.17.cloned.1.call-update) | async-done | bytes 2097168 | tf_op jit(solution)/shard_map/all_gather | solution.py:163
  322.1 14.7 %convolution_convert_fusion = bf16[2048,2048]{1,0:T(8,128)(2,1)} fusion(bf16[512,2048]{1,0:T(8,128)(2,1)} %all-gather.17.cloned.1.call-done, f32[2048,512]{1,0:T(8,128)} %fusion.30, bf16[2048,2048]{1,0:T(8,128)(2,1)} %all-gather.13.cloned.1.call-done, bf16[2048,512]{1,0:T(8,128)(2,1)S(1)} %bitcast.115), kind=kOutput, calls=%fused_computation.25 | convolution fusion | flops 8600420352 | bytes 25165824 | tf_op jit(solution)/shard_map/dot_general | solution.py:170
  336.8 87.0 %reduce-scatter.2.cloned.1.call-done = bf16[128,2048]{1,0:T(8,128)(2,1)} async-done(((bf16[2048,2048]{1,0:T(8,128)(2,1)}), bf16[128,2048]{1,0:T(8,128)(2,1)}) %reduce-scatter.2.cloned.1.call-update) | async-done | bytes 524304 | tf_op jit(solution)/shard_map/reduce_scatter | solution.py:169
  423.7 1.9 add_convert_fusion
  (136 shorter events, 36.2 us)
Async XLA Ops:
  6.5 62.4 %all-gather.9.cloned.1.call-start = ((), (), s32[]{:S(2)}) async-start(), calls=%async_computation.6 | async-start | bytes 4456448 | tf_op jit(solution)/shard_map/all_gather | solution.py:96
  8.4 157.6 %all-gather.11.cloned.1.call-start = ((), (), s32[]{:S(2)}) async-start(), calls=%async_computation.7 | async-start | bytes 1114112 | tf_op jit(solution)/shard_map/all_gather | solution.py:98
  9.1 156.8 %all-gather.7.cloned.1.call-start = ((), (), s32[]{:S(2)}) async-start(), calls=%async_computation.5 | async-start | bytes 1114112 | tf_op jit(solution)/shard_map/all_gather | solution.py:97
  74.1 3.2 copy-start
  74.1 3.2 copy-start.2
  90.4 3.2 copy-start
  90.4 3.2 copy-start.2
  106.6 3.2 copy-start
  106.6 3.2 copy-start.2
  122.8 3.2 copy-start
  122.9 3.2 copy-start.2
  134.6 12.9 %all-to-all-start = ((f32[16,128,16]{1,2,0:T(8,128)}), f32[16,128,16]{1,2,0:T(8,128)S(1)}, u32[]{:S(2)}, u32[]{:S(2)}) async-start(f32[16,128,16]{1,2,0:T(8,128)} %copy.66), calls=%async_computation | async-start | bytes 262144 | tf_op jit(solution)/shard_map/all_to_all | solution.py:138
  147.6 11.8 %all-to-all-start.1 = ((f32[16,128,16]{1,2,0:T(8,128)}), f32[16,128,16]{1,2,0:T(8,128)S(1)}, u32[]{:S(2)}, u32[]{:S(2)}) async-start(f32[16,128,16]{1,2,0:T(8,128)} %copy.70), calls=%async_computation.1 | async-start | bytes 262144 | tf_op jit(solution)/shard_map/all_to_all | solution.py:139
  157.5 9.4 %copy-start.6 = (bf16[128,256]{1,0:T(8,128)(2,1)S(1)}, bf16[128,256]{1,0:T(8,128)(2,1)}, u32[]{:S(2)}) copy-start(bf16[128,256]{1,0:T(8,128)(2,1)} %param.18) | copy-start | bytes 196612
  157.5 9.5 %copy-start.7 = (bf16[128,256]{1,0:T(8,128)(2,1)S(1)}, bf16[128,256]{1,0:T(8,128)(2,1)}, u32[]{:S(2)}) copy-start(bf16[128,256]{1,0:T(8,128)(2,1)} %param.19) | copy-start | bytes 196612
  157.5 9.7 %copy-start.3 = (bf16[128,1024]{0,1:T(8,128)(2,1)S(1)}, bf16[128,1024]{0,1:T(8,128)(2,1)}, u32[]{:S(2)}) copy-start(bf16[128,1024]{0,1:T(8,128)(2,1)} %copy.63) | copy-start | bytes 786436
  159.4 59.6 %all-to-all-start.2 = ((bf16[16,128,1024]{1,2,0:T(8,128)(2,1)}), bf16[16,128,1024]{1,2,0:T(8,128)(2,1)}, u32[]{:S(2)}, u32[]{:S(2)}) async-start(bf16[16,128,1024]{1,2,0:T(8,128)(2,1)} %copy.75), calls=%async_computation.2 | async-start | bytes 8388608 | tf_op jit(solution)/shard_map/all_to_all | solution.py:136
  164.9 66.2 %all-gather.15.cloned.1.call-start = ((), (), s32[]{:S(2)}) async-start(), calls=%async_computation.9 | async-start | bytes 2359296 | tf_op jit(solution)/shard_map/all_gather | solution.py:159
  165.4 128.8 %all-gather.13.cloned.1.call-start = ((), (), s32[]{:S(2)}) async-start(), calls=%async_computation.8 | async-start | bytes 8912896 | tf_op jit(solution)/shard_map/all_gather | solution.py:165
  168.3 54.4 %copy-start.4 = (bf16[128,2048]{1,0:T(8,128)(2,1)S(1)}, bf16[128,2048]{1,0:T(8,128)(2,1)}, u32[]{:S(2)}) copy-start(bf16[128,2048]{1,0:T(8,128)(2,1)} %param.16) | copy-start | bytes 1572868
  219.0 3.7 copy-start.1
  222.7 0.9 copy-start.8
  222.8 2.4 copy-start.5
  224.6 97.5 %all-gather.17.cloned.1.call-start = ((), (), s32[]{:S(2)}) async-start(), calls=%async_computation.10 | async-start | bytes 2359296 | tf_op jit(solution)/shard_map/all_gather | solution.py:163
  226.7 78.0 %all-to-all-start.3 = ((bf16[8,256,512]{2,1,0:T(8,128)(2,1)}), bf16[8,256,512]{2,1,0:T(8,128)(2,1)S(1)}, u32[]{:S(2)}, u32[]{:S(2)}) async-start(bf16[8,256,512]{2,1,0:T(8,128)(2,1)} %stack.2), calls=%async_computation.3 | async-start | bytes 4194304 | tf_op jit(solution)/shard_map/all_to_all | solution.py:161
  231.0 192.8 %reduce-scatter.2.cloned.1.call-start = ((), (), s32[]{:S(2)}) async-start(), calls=%async_computation.11 | async-start | bytes 8912896 | tf_op jit(solution)/shard_map/reduce_scatter | solution.py:169
Sparse Core Ops, SparseCore 0:
  9.4 59.4 all-gather.8
  71.1 41.8 all-gather.10
  115.2 42.2 all-gather.6
  167.1 26.6 all-gather.14
  224.7 69.4 all-gather.12
  295.7 26.3 all-gather.16
  336.9 86.7 reduce-scatter.1
